TPU v7x, 512 devices: a whole 4x4x16 slice. The times are simulated.
512 devices in a mesh: seq: 16 (over x, y_hi, core), head: 32 (over z, y_lo).
Axes of the slice: x: 4, y: 4 (y_hi: 2, y_lo: 2; y = y_hi * 2 + y_lo), z: 16, core: 2. Of those that a mesh axis runs over, the one named last changes fastest.
Arguments:
- x_inner: bfloat16 [24576, 16384], P('seq', 'head'), may hold values from -400 to 400
- z_gate: bfloat16 [24576, 16384], P('seq', 'head'), may hold values from -6 to 6
- bc_raw: bfloat16 [24576, 512], P(('seq', 'head')), may hold values from -6 to 6
- conv_weight: float32 [4, 512], replicated, may hold values from -3 to 3
- conv_bias: float32 [512], replicated, may hold values from -3 to 3
- dt_raw: float32 [24576, 128], P('seq', 'head'), may hold values from -6 to 24576
- a_log: float32 [128], P('head'), may hold values from -20 to 1
- d_skip: float32 [128], P('head'), may hold values from 0.5 to 1.5
- norm_gain: float32 [16384], P('head'), may hold values from 0.5 to 1.5
Outputs:
- mixer_out: bfloat16 [24576, 16384], P('seq', 'head')
All inputs are finite; a program needn't handle non-finite values.
Results may differ from a plain program's by a relative error of at most 0.0034.
Values may be sent and summed in bfloat16 or wider, within the bound.
A program may use at most 64 MiB of HBM per device.

v0:
```python
import jax
import jax.numpy as jnp
from jax import lax
from jax.sharding import PartitionSpec as P

HEAD_DIM = 128
STATE = 256
BLOCK = 256
INNER = 16384


def shifted(shard, axis, by):
    length = lax.axis_size(axis)
    pairs = [(i, i + by) for i in range(length) if 0 <= i + by < length]
    return lax.ppermute(shard, axis, pairs)


def prefix(part, axis, combine, identity):
    place = lax.axis_index(axis)
    gathered = jax.tree.map(lambda a: lax.all_gather(a, axis), part)
    state = jax.tree.map(lambda a, e: jnp.zeros_like(a) + jnp.asarray(e, a.dtype), part, identity)

    def one(hop, state):
        return combine(
            state, jax.tree.map(lambda a: lax.dynamic_index_in_dim(a, hop, 0, False), gathered)
        )

    return lax.fori_loop(0, place, one, state)


def convolve_rows(padded, conv_weight, conv_bias):
    tap_count = conv_weight.shape[0]
    row_count = padded.shape[0] - tap_count + 1
    padded_float = padded.astype(jnp.float32)
    accumulated = jnp.broadcast_to(conv_bias[None, :], (row_count, padded.shape[1]))
    for offset in range(tap_count):
        accumulated = (
            accumulated + conv_weight[offset][None, :] * padded_float[offset : offset + row_count]
        )
    return jax.nn.silu(accumulated).astype(jnp.bfloat16)


def on_device(x_inner, z_gate, bc_raw, conv_weight, conv_bias, dt_raw, a_log, d_skip, norm_gain):
    highest = lax.Precision.HIGHEST
    rim_count = conv_weight.shape[0] - 1
    gathered = lax.all_gather(bc_raw, "head", axis=0, tiled=True)
    rim_rows = shifted(gathered[-rim_count:], "seq", 1)
    bc_act = convolve_rows(jnp.concatenate([rim_rows, gathered], axis=0), conv_weight, conv_bias)
    length = x_inner.shape[0]
    head_count = a_log.shape[0]
    block_count = length // BLOCK
    step_size = jax.nn.softplus(dt_raw)
    log_step = -jnp.exp(a_log)[None, :] * step_size
    cum_log = jnp.cumsum(log_step.reshape(block_count, BLOCK, head_count), axis=1)
    size_blocks = step_size.reshape(block_count, BLOCK, head_count)
    b_blocks = bc_act[:, :STATE].reshape(block_count, BLOCK, STATE)
    c_blocks = bc_act[:, STATE:].reshape(block_count, BLOCK, STATE)
    x_float = x_inner.astype(jnp.float32).reshape(block_count, BLOCK, head_count, HEAD_DIM)
    gram_blocks = jnp.einsum("cin,cjn->cij", c_blocks, b_blocks, preferred_element_type=jnp.float32)
    lower_mask = jnp.tril(jnp.ones((BLOCK, BLOCK), dtype=bool))
    by_head = jnp.transpose(cum_log, (0, 2, 1))
    spread = by_head[:, :, :, None] - by_head[:, :, None, :]
    decay_blocks = jnp.where(lower_mask, jnp.exp(jnp.where(lower_mask, spread, 0.0)), 0.0)
    weights = (
        gram_blocks[:, None] * decay_blocks * jnp.transpose(size_blocks, (0, 2, 1))[:, :, None, :]
    )
    inner_part = jnp.einsum("chij,cjhp->cihp", weights, x_float, precision=highest)
    tail_weight = jnp.exp(cum_log[:, -1:, :] - cum_log) * size_blocks
    block_states = jnp.einsum(
        "cjhp,cjn->chpn",
        x_float * tail_weight[..., None],
        b_blocks.astype(jnp.float32),
        precision=highest,
    )
    block_decay = jnp.exp(cum_log[:, -1, :])
    zero_state = jnp.zeros((head_count, HEAD_DIM, STATE), jnp.float32)
    starts = []
    current = zero_state
    for block_index in range(block_count):
        starts.append(current)
        current = block_decay[block_index][:, None, None] * current + block_states[block_index]
    zero_starts = jnp.stack(starts)
    log_total = jnp.sum(cum_log[:, -1, :], axis=0)

    def combine(earlier, later):
        return (earlier[0] + later[0], jnp.exp(later[0])[:, None, None] * earlier[1] + later[1])

    identity = (jnp.zeros_like(log_total), zero_state)
    chained = prefix((log_total, current), "seq", combine, identity)
    incoming = chained[1]
    c_float = c_blocks.astype(jnp.float32)
    carried_part = jnp.exp(cum_log)[..., None] * jnp.einsum(
        "cin,chpn->cihp", c_float, zero_starts, precision=highest
    )
    prior_log = jnp.cumsum(cum_log[:, -1, :], axis=0) - cum_log[:, -1, :]
    entry_part = jnp.exp(cum_log + prior_log[:, None, :])[..., None] * jnp.einsum(
        "cin,hpn->cihp", c_float, incoming, precision=highest
    )
    carried_part = carried_part + entry_part
    ssm_out = inner_part + carried_part + d_skip[None, None, :, None] * x_float
    gated_out = ssm_out.reshape(length, head_count * HEAD_DIM) * jax.nn.silu(
        z_gate.astype(jnp.float32)
    )
    square_sum = lax.psum(jnp.sum(gated_out * gated_out, axis=1), "head")
    inverse_rms = lax.rsqrt(square_sum / INNER + 1e-05)
    return (gated_out * inverse_rms[:, None] * norm_gain[None, :]).astype(jnp.bfloat16)


def solution(mesh):
    placed = (
        P("seq", "head"),
        P("seq", "head"),
        P(("seq", "head"), None),
        P(),
        P(),
        P("seq", "head"),
        P("head"),
        P("head"),
        P("head"),
    )
    return jax.shard_map(
        on_device, mesh=mesh, in_specs=placed, out_specs=P("seq", "head"), check_vma=False
    )
```

profile of v0, /device:TPU:22, one launch (start us, length us, event | category | flops | bytes accessed | tf_op | source)
XLA Modules:
  0.0 351.3 jit_solution(10148498477770559478)
XLA Ops:
  6.5 0.7 all-gather.4.cloned.1.call-update
  7.3 0.7 exponential_negate_fusion
  8.0 0.8 broadcast_multiply_fusion
  8.8 7.2 %reduce-window.6 = f32[6,4,2,128]{3,2,1,0:T(2,128)S(1)} reduce-window(f32[6,4,2,128]{3,2,1,0:T(2,128)S(1)} %copy.59, f32[]{:T(128)} %constant.42.clone.1), window={size=1x1x1x128 pad=0_0x0_0x0_0x127_0}, to_apply=%region_0.1 | reduce-window | flops 780288 | bytes 49156 | tf_op jit(solution)/shard_map/reduce-window
  16.7 0.2 subtract_reduce_fusion
  16.9 0.8 broadcast_dynamic-update-slice_fusion
  17.7 0.9 fusion.36
  18.7 127.5 %all-gather.4.cloned.1.call-done = bf16[1536,512]{1,0:T(8,128)(2,1)} async-done(((bf16[48,512]{1,0:T(8,128)(2,1)}), bf16[1536,512]{1,0:T(8,128)(2,1)}) %all-gather.4.cloned.1.call-update) | async-done | bytes 1572880 | tf_op jit(solution)/shard_map/all_gather | solution.py:46
  146.2 0.8 slice.108
  147.1 1.9 collective-permute-start
  149.0 0.3 slice_reduce_fusion.1
  149.2 2.4 reshape.86
  151.6 1.8 collective-permute-done
  153.5 0.5 maximum_convert_fusion
  154.0 2.0 multiply_convert_fusion.1
  156.1 4.3 %fusion.7 = f32[6,4,128,256]{3,2,1,0:T(8,128)S(1)} fusion(bf16[6,256,256,1]{2,1,3,0:T(8,128)(2,1)S(1)} %bitcast.69, f32[6,256,4]{1,2,0:T(4,128)S(1)} %copy.52, bf16[6,256,4,128]{3,2,1,0:T(4,128)(2,1)S(1)} %reshape.86), kind=kOutput, calls=%fused_computation.13 | convolution fusion | flops 2417491968 | bytes 5529600 | tf_op jit(solution)/shard_map/cjhp,cjn->chpn/dot_general | solution.py:69
  160.5 0.1 constant_dynamic-update-slice_fusion.1
  160.8 0.2 constant_dynamic-update-slice_fusion
  161.0 1.0 fusion.30
  162.0 1.8 copy-done.2
  163.8 1.3 dynamic-slice
  165.7 0.2 dynamic-update-slice
  165.9 27.4 %all-reduce = f32[64]{0:T(128)S(1)} all-reduce(f32[64]{0:T(128)S(1)} %dynamic-update-slice), channel_id=2, replica_groups=mesh['seq'=16,'head'=32] {'seq'}, use_global_device_ids=true, to_apply=%add | all-reduce | flops 64 | bytes 512
  193.5 0.4 fusion.37
  193.9 6.0 %fusion = f32[6,4,256,128]{3,2,1,0:T(8,128)} fusion(f32[6,4,256]{2,1,0:T(4,128)S(1)} %copy.47, f32[6,4,256]{2,1,0:T(4,128)S(1)} %reduce_window_sum.35, f32[6,256,256]{2,1,0:T(8,128)S(1)} %fusion.37, pred[256,256]{1,0:T(8,128)(4,1)S(1)} %iota_compare_fusion, bf16[6,256,4,128]{3,2,1,0:T(4,128)(2,1)S(1)} %reshape.86), kind=kOutput, calls=%fused_computation.2 | convolution fusion | flops 2423783424 | bytes 6406144 | tf_op jit(solution)/shard_map/chij,cjhp->cihp/dot_general | solution.py:67
  199.9 46.5 %all-gather.6.cloned.1.call-done = f32[16,4,128,256]{3,2,1,0:T(8,128)} async-done(((f32[1,4,128,256]{3,2,1,0:T(8,128)}), f32[16,4,128,256]{3,2,1,0:T(8,128)}) %all-gather.6.cloned.1.call-update) | async-done | bytes 8388624 | tf_op jit(solution)/shard_map/all_gather | solution.py:20
  246.4 17.7 %while.12 = (s32[]{:T(128)}, f32[4,128,256]{2,1,0:T(8,128)S(1)}, s32[]{:T(128)}, f32[16,4]{1,0:T(8,128)S(1)}, f32[16,4,128,256]{3,2,1,0:T(8,128)}, /*index=5*/s32[]{:T(128)}, s32[]{:T(128)}, s32[]{:T(128)}) while((s32[]{:T(128)}, f32[4,128,256]{2,1,0:T(8,128)S(1)}, s32[]{:T(128)}, f32[16,4]{1,0:T(8,128)S(1)}, f32[16,4,128,256]{3,2,1,0:T(8,128)}, ...), condition=%wide.region_5.6_spmd, body=%wide.region_4.5_spmd.sunk | while | flops 262149 | bytes 1573039 | solution.py:28
  246.5 1.2 bitcast_add_fusion.3
  247.7 1.2 bitcast_add_fusion.3
  249.0 1.2 bitcast_add_fusion.3
  250.2 1.2 bitcast_add_fusion.3
  251.5 1.2 bitcast_add_fusion.3
  252.7 1.2 bitcast_add_fusion.3
  254.0 1.2 bitcast_add_fusion.3
  255.2 1.2 bitcast_add_fusion.3
  256.5 1.2 bitcast_add_fusion.3
  257.7 1.2 bitcast_add_fusion.3
  259.0 1.2 bitcast_add_fusion.3
  260.2 1.2 bitcast_add_fusion.3
  261.5 1.2 bitcast_add_fusion.3
  262.7 1.2 bitcast_add_fusion.3
  264.1 1.5 fusion.26
  265.6 0.4 copy-done.3
  266.0 5.3 %fusion.8 = f32[6,256,4,128]{3,1,2,0:T(8,128)S(1)} fusion(f32[6,4,256,128]{3,2,1,0:T(8,128)} %fusion, f32[6,256,4,128]{3,1,2,0:T(8,128)S(1)} %fusion.26, bf16[6,256,256,1]{2,1,3,0:T(8,128)(2,1)S(1)} %bitcast.68, f32[6,4,128,256]{3,2,1,0:T(8,128)S(1)} %copy-done.3, f32[4]{0:T(128)S(1)} %copy-done.7, f32[6,256,4]{1,2,0:T(4,128)S(1)} %copy.54, ...), kind=kOutput, calls=%fused_computation.14 | convolution fusion | flops 2421424128 | bytes 14991376 | tf_op jit(solution)/shard_map/cin,chpn->cihp/dot_general | solution.py:92
  271.3 2.0 copy.55
  273.4 1.0 multiply_reduce_fusion
  274.4 66.5 %psum.7 = f32[1536]{0:T(1024)S(1)} all-reduce(f32[1536]{0:T(1024)S(1)} %multiply_reduce_fusion), channel_id=1, replica_groups=mesh['seq'=16,'head'=32] {'head'}, use_global_device_ids=true, to_apply=%region_7.8 | all-reduce | flops 1536 | bytes 12288 | tf_op jit(solution)/shard_map/psum | solution.py:104
  341.0 3.5 multiply_convert_fusion
  (59 shorter events, 1.6 us)
Async XLA Ops:
  6.5 139.7 %all-gather.4.cloned.1.call-start = ((), (), s32[]{:S(2)}) async-start(), calls=%async_computation | async-start | bytes 1622016 | tf_op jit(solution)/shard_map/all_gather | solution.py:46
  7.3 239.1 %all-gather.6.cloned.1.call-start = ((), (), s32[]{:S(2)}) async-start(), calls=%async_computation.1 | async-start | bytes 8912896 | tf_op jit(solution)/shard_map/all_gather | solution.py:20
  146.2 7.2 %copy-start.4 = (bf16[1536,512]{1,0:T(8,128)(2,1)S(1)}, bf16[1536,512]{1,0:T(8,128)(2,1)}, u32[]{:S(2)}) copy-start(bf16[1536,512]{1,0:T(8,128)(2,1)} %all-gather.4.cloned.1.call-done) | copy-start | bytes 4718596
  147.1 6.4 %collective-permute-start = (bf16[3,512]{1,0:T(4,128)(2,1)S(1)}, bf16[3,512]{1,0:T(4,128)(2,1)S(1)}, u32[]{:S(2)}, u32[]{:S(2)}) collective-permute-start(bf16[3,512]{1,0:T(4,128)(2,1)S(1)} %slice.108), channel_id=1, source_target_pairs={{0,32},{32,64},{64,96},{96,128},{128,160},{160,192},{192,224},{224... | collective-permute-start | bytes 9224 | tf_op jit(solution)/shard_map/ppermute | solution.py:15
  151.6 2.3 copy-start.5
  156.1 4.3 %copy-start.1 = (f32[6,4,128,256]{3,2,1,0:T(8,128)S(1)}, f32[6,4,128,256]{3,2,1,0:T(8,128)}, u32[]{:S(2)}) copy-start(f32[6,4,128,256]{3,2,1,0:T(8,128)} %broadcast_dynamic-update-slice_fusion) | copy-start | bytes 9437188
  162.0 1.8 copy-start.2
  264.1 1.9 copy-start.3
  264.1 1.9 copy-start.7
  271.3 2.1 copy-start
  273.3 67.6 %copy-start.6 = (f32[512]{0:T(512)S(1)}, f32[512]{0:T(512)}, u32[]{:S(2)}) copy-start(f32[512]{0:T(512)} %param.19) | copy-start | bytes 6148
Sparse Core Ops, SparseCore 0:
  9.4 136.7 all-gather.3
  163.9 82.4 all-gather.5
where the time goes:
time: 352 us; the launch traced here: 351 us
  waiting for transfers between devices  177 us (50%)
  blocking collectives  93.9 us (27%)
  other arithmetic  34.8 us (10%)
  matrix products  17.5 us (5%)
  between operations  14.4 us (4%)
  local copies, waits for them, and re-layouts  11.6 us (3%)
    all_gather x1, waiting for transfers between devices, on_device(): gathered = lax.all_gather(bc_raw, 'head', axis=0, tiled=True)  128 us
    psum x1, blocking collectives, on_device(): square_sum = lax.psum(jnp.sum(gated_out * gated_out, axis=1), 'head')  66.5 us
    all_gather x1, waiting for transfers between devices, prefix(): gathered = jax.tree.map(lambda a: lax.all_gather(a, axis), part)  46.5 us
    unnamed x1, blocking collectives  27.4 us
    add x14, other arithmetic, combine(): jnp.exp(later[0])[:, None, None] * earlier[1] + later[1]  16.8 us
    another operation x3, other arithmetic  7.34 us
  transfers between devices with their start and end apart: 3, of which 3 were waited for; matrix products, arithmetic and copies ran while one was open for 6% of the time, Pallas kernels for 0%

commit v1 on v0

--- a/solution.py
+++ b/solution.py
@@ -41,6 +41,11 @@
 
 
 def on_device(x_inner, z_gate, bc_raw, conv_weight, conv_bias, dt_raw, a_log, d_skip, norm_gain):
+
+    def render_space(base_x, link_axis):
+        base_arr = lax.all_gather(base_x, link_axis)
+        return jnp.sum(base_arr, axis=0)
+
     highest = lax.Precision.HIGHEST
     rim_count = conv_weight.shape[0] - 1
     gathered = lax.all_gather(bc_raw, "head", axis=0, tiled=True)
@@ -101,7 +106,7 @@
     gated_out = ssm_out.reshape(length, head_count * HEAD_DIM) * jax.nn.silu(
         z_gate.astype(jnp.float32)
     )
-    square_sum = lax.psum(jnp.sum(gated_out * gated_out, axis=1), "head")
+    square_sum = render_space(jnp.sum(gated_out * gated_out, axis=1), "head")
     inverse_rms = lax.rsqrt(square_sum / INNER + 1e-05)
     return (gated_out * inverse_rms[:, None] * norm_gain[None, :]).astype(jnp.bfloat16)
 

time: 352 us -> 352 us (level)
    psum x1 -> x0, blocking collectives: 66.5 us -> none  [on_device(): square_sum = lax.psum(jnp.sum(gated_out * gated_out, axis=1), 'head')]
    all_gather x0 -> x1, blocking collectives: none -> 65 us  [render_space(): base_arr = lax.all_gather(base_x, link_axis)]
  transfers between devices with their start and end apart: 3 -> 3, of which waited for: 3 -> 3; matrix products, arithmetic and copies ran while one was open for 6% -> 7% of each run, Pallas kernels for 0% -> 0%
where the time goes in v1:
time: 352 us; the launch traced here: 351 us
  waiting for transfers between devices  175 us (50%)
  blocking collectives  92.4 us (26%)
  other arithmetic  36.3 us (10%)
  matrix products  18.7 us (5%)
  between operations  14.4 us (4%)
  local copies, waits for them, and re-layouts  11.5 us (3%)
    all_gather x1, waiting for transfers between devices, on_device(): gathered = lax.all_gather(bc_raw, 'head', axis=0, tiled=True)  128 us
    all_gather x1, blocking collectives, render_space(): base_arr = lax.all_gather(base_x, link_axis)  65 us
    all_gather x1, waiting for transfers between devices, prefix(): gathered = jax.tree.map(lambda a: lax.all_gather(a, axis), part)  45.3 us
    unnamed x1, blocking collectives  27.4 us
    add x14, other arithmetic, combine(): jnp.exp(later[0])[:, None, None] * earlier[1] + later[1]  16.8 us
    another operation x3, other arithmetic  7.34 us
  transfers between devices with their start and end apart: 3, of which 3 were waited for; matrix products, arithmetic and copies ran while one was open for 7% of the time, Pallas kernels for 0%

profile of v1, /device:TPU:22, one launch (start us, length us, event | category | flops | bytes accessed | tf_op | source)
XLA Modules:
  0.0 351.3 jit_solution(9306907876210233286)
XLA Ops:
  6.5 0.7 all-gather.6.cloned.1.call-update
  7.3 0.7 exponential_negate_fusion
  8.0 0.8 broadcast_multiply_fusion
  8.8 7.2 %reduce-window.6 = f32[6,4,2,128]{3,2,1,0:T(2,128)S(1)} reduce-window(f32[6,4,2,128]{3,2,1,0:T(2,128)S(1)} %copy.59, f32[]{:T(128)} %constant.42.clone.1), window={size=1x1x1x128 pad=0_0x0_0x0_0x127_0}, to_apply=%region_0.1 | reduce-window | flops 780288 | bytes 49156 | tf_op jit(solution)/shard_map/reduce-window
  16.7 0.2 subtract_reduce_fusion
  16.9 0.8 broadcast_dynamic-update-slice_fusion
  17.7 0.9 fusion.36
  18.7 127.5 %all-gather.6.cloned.1.call-done = bf16[1536,512]{1,0:T(8,128)(2,1)} async-done(((bf16[48,512]{1,0:T(8,128)(2,1)}), bf16[1536,512]{1,0:T(8,128)(2,1)}) %all-gather.6.cloned.1.call-update) | async-done | bytes 1572880 | tf_op jit(solution)/shard_map/all_gather | solution.py:51
  146.2 0.7 slice.108
  146.9 1.9 collective-permute-start
  148.8 0.3 slice_reduce_fusion.1
  149.1 2.4 reshape.90
  151.5 1.8 collective-permute-done
  153.4 1.9 maximum_convert_fusion
  155.2 2.0 multiply_convert_fusion.1
  157.4 4.4 %fusion.7 = f32[6,4,128,256]{3,2,1,0:T(8,128)S(1)} fusion(bf16[6,256,256,1]{2,1,3,0:T(8,128)(2,1)S(1)} %bitcast.69, f32[6,256,4]{1,2,0:T(4,128)S(1)} %copy.52, bf16[6,256,4,128]{3,2,1,0:T(4,128)(2,1)S(1)} %reshape.90), kind=kOutput, calls=%fused_computation.13 | convolution fusion | flops 2417491968 | bytes 5529600 | tf_op jit(solution)/shard_map/cjhp,cjn->chpn/dot_general | solution.py:74
  161.9 0.1 constant_dynamic-update-slice_fusion.1
  162.2 0.2 constant_dynamic-update-slice_fusion
  162.4 1.0 fusion.30
  163.4 1.8 copy-done.3
  165.2 1.3 dynamic-slice
  167.1 0.2 dynamic-update-slice
  167.3 27.4 %all-reduce = f32[64]{0:T(128)S(1)} all-reduce(f32[64]{0:T(128)S(1)} %dynamic-update-slice), channel_id=2, replica_groups=mesh['seq'=16,'head'=32] {'seq'}, use_global_device_ids=true, to_apply=%add | all-reduce | flops 64 | bytes 512
  194.9 1.5 fusion.37
  196.4 6.0 %fusion = f32[6,4,256,128]{3,2,1,0:T(8,128)} fusion(f32[6,4,256]{2,1,0:T(4,128)S(1)} %copy.47, f32[6,4,256]{2,1,0:T(4,128)S(1)} %reduce_window_sum.35, f32[6,256,256]{2,1,0:T(8,128)S(1)} %fusion.37, pred[256,256]{1,0:T(8,128)(4,1)S(1)} %iota_compare_fusion, bf16[6,256,4,128]{3,2,1,0:T(4,128)(2,1)S(1)} %reshape.90), kind=kOutput, calls=%fused_computation.2 | convolution fusion | flops 2423783424 | bytes 6406144 | tf_op jit(solution)/shard_map/chij,cjhp->cihp/dot_general | solution.py:72
  202.4 45.3 %all-gather.8.cloned.1.call-done = f32[16,4,128,256]{3,2,1,0:T(8,128)} async-done(((f32[1,4,128,256]{3,2,1,0:T(8,128)}), f32[16,4,128,256]{3,2,1,0:T(8,128)}) %all-gather.8.cloned.1.call-update) | async-done | bytes 8388624 | tf_op jit(solution)/shard_map/all_gather | solution.py:20
  247.8 17.7 %while.12 = (s32[]{:T(128)}, f32[4,128,256]{2,1,0:T(8,128)S(1)}, s32[]{:T(128)}, f32[16,4]{1,0:T(8,128)S(1)}, f32[16,4,128,256]{3,2,1,0:T(8,128)}, /*index=5*/s32[]{:T(128)}, s32[]{:T(128)}, s32[]{:T(128)}) while((s32[]{:T(128)}, f32[4,128,256]{2,1,0:T(8,128)S(1)}, s32[]{:T(128)}, f32[16,4]{1,0:T(8,128)S(1)}, f32[16,4,128,256]{3,2,1,0:T(8,128)}, ...), condition=%wide.region_5.6_spmd, body=%wide.region_4.5_spmd.sunk | while | flops 262149 | bytes 1573039 | solution.py:28
  247.9 1.2 bitcast_add_fusion.3
  249.1 1.2 bitcast_add_fusion.3
  250.4 1.2 bitcast_add_fusion.3
  251.6 1.2 bitcast_add_fusion.3
  252.9 1.2 bitcast_add_fusion.3
  254.1 1.2 bitcast_add_fusion.3
  255.4 1.2 bitcast_add_fusion.3
  256.6 1.2 bitcast_add_fusion.3
  257.9 1.2 bitcast_add_fusion.3
  259.1 1.2 bitcast_add_fusion.3
  260.4 1.2 bitcast_add_fusion.3
  261.6 1.2 bitcast_add_fusion.3
  262.9 1.2 bitcast_add_fusion.3
  264.1 1.2 bitcast_add_fusion.3
  265.5 1.5 fusion.26
  267.0 0.4 copy-done.4
  267.4 5.3 %fusion.8 = f32[6,256,4,128]{3,1,2,0:T(8,128)S(1)} fusion(f32[6,4,256,128]{3,2,1,0:T(8,128)} %fusion, f32[6,256,4,128]{3,1,2,0:T(8,128)S(1)} %fusion.26, bf16[6,256,256,1]{2,1,3,0:T(8,128)(2,1)S(1)} %bitcast.68, f32[6,4,128,256]{3,2,1,0:T(8,128)S(1)} %copy-done.4, f32[4]{0:T(128)S(1)} %copy-done.7, f32[6,256,4]{1,2,0:T(4,128)S(1)} %copy.54, ...), kind=kOutput, calls=%fused_computation.14 | convolution fusion | flops 2421424128 | bytes 14991376 | tf_op jit(solution)/shard_map/cin,chpn->cihp/dot_general | solution.py:97
  272.7 2.0 copy.55
  274.8 1.0 multiply_reduce_fusion
  275.8 65.0 %all-gather.2 = f32[32,1,1536]{2,1,0:T(1,128)S(1)} all-gather(f32[1,1,1536]{2,1,0:T(1,128)S(1)} %reshape.98), channel_id=3, replica_groups=mesh['seq'=16,'head'=32] {'head'}, dimensions={0}, use_global_device_ids=true | all-gather | bytes 202752 | tf_op jit(solution)/shard_map/all_gather | solution.py:46
  340.9 3.5 multiply_convert_fusion
  (61 shorter events, 1.7 us)
Async XLA Ops:
  6.5 139.7 %all-gather.6.cloned.1.call-start = ((), (), s32[]{:S(2)}) async-start(), calls=%async_computation | async-start | bytes 1622016 | tf_op jit(solution)/shard_map/all_gather | solution.py:51
  7.3 240.5 %all-gather.8.cloned.1.call-start = ((), (), s32[]{:S(2)}) async-start(), calls=%async_computation.1 | async-start | bytes 8912896 | tf_op jit(solution)/shard_map/all_gather | solution.py:20
  146.9 6.4 %collective-permute-start = (bf16[3,512]{1,0:T(4,128)(2,1)S(1)}, bf16[3,512]{1,0:T(4,128)(2,1)S(1)}, u32[]{:S(2)}, u32[]{:S(2)}) collective-permute-start(bf16[3,512]{1,0:T(4,128)(2,1)S(1)} %slice.108), channel_id=1, source_target_pairs={{0,32},{32,64},{64,96},{96,128},{128,160},{160,192},{192,224},{224... | collective-permute-start | bytes 9224 | tf_op jit(solution)/shard_map/ppermute | solution.py:15
  151.5 3.7 %copy-start.5 = (f32[512]{0:T(512)S(1)}, f32[512]{0:T(512)}, u32[]{:S(2)}) copy-start(f32[512]{0:T(512)} %param.15) | copy-start | bytes 6148
  157.4 6.0 %copy-start = (bf16[1536,256]{1,0:T(8,128)(2,1)}, bf16[1536,256]{1,0:T(8,128)(2,1)S(1)}, u32[]{:S(2)}) copy-start(bf16[1536,256]{1,0:T(8,128)(2,1)S(1)} %get-tuple-element.75) | copy-start | bytes 2359300
  157.4 4.4 %copy-start.2 = (f32[6,4,128,256]{3,2,1,0:T(8,128)S(1)}, f32[6,4,128,256]{3,2,1,0:T(8,128)}, u32[]{:S(2)}) copy-start(f32[6,4,128,256]{3,2,1,0:T(8,128)} %broadcast_dynamic-update-slice_fusion) | copy-start | bytes 9437188
  163.4 1.8 copy-start.3
  265.5 1.9 copy-start.4
  265.5 1.9 copy-start.7
  272.7 2.1 copy-start.1
  274.7 66.2 %copy-start.6 = (f32[512]{0:T(512)S(1)}, f32[512]{0:T(512)}, u32[]{:S(2)}) copy-start(f32[512]{0:T(512)} %param.19) | copy-start | bytes 6148
Sparse Core Ops, SparseCore 0:
  9.4 136.7 all-gather.5
  165.3 82.4 all-gather.7
